TPU v7x, 512 devices: a whole 4x8x8 slice. The times are simulated.
512 devices in a mesh: expert: 32 (over y, x), tensor: 16 (over z, core).
Axes of the slice: x: 4, y: 8, z: 8, core: 2. Of those that a mesh axis runs over, the one named last changes fastest.
Arguments:
- residual: bfloat16 [2048, 7168], P('expert', 'tensor'), may hold values from -40 to 40
- attn_parts: bfloat16 [16, 2048, 7168], P('tensor', 'expert'), may hold values from -2 to 2
- norm_gain: bfloat16 [7168], P('tensor'), may hold values from 0.099609375 to 1.8984375
- routes: int32 [2048, 8], P('expert'), may hold values from 0 to 31, all different within a row; in each aligned block of 64 rows (0 to 63, 64 to 127, ...) at most 24 rows name the same one
- route_weights: float32 [2048, 8], P('expert'), may hold values from 0.05 to 0.6
- w_gate: bfloat16 [32, 7168, 2048], P('expert', None, 'tensor'), may hold values from -0.06023809 to 0.06023809
- w_gate_q: bfloat16 [32, 7168, 2048], P('expert', None, 'tensor'), may hold values from -0.09567226 to 0.09567226
Outputs:
- token_error: float32 [2048], P('expert')
- expert_error: float32 [32], P('expert')
- hess_diag: float32 [32, 7168], P('expert', 'tensor')
Inputs may be any that keep to these rules, and one draw needn't show every extreme that they name: `routes`: no expert is named by more than 24 of the rows of one device, and in every draw some expert is named by exactly 24 of them; the 8 experts of a token are distinct; every expert is named by some token.
All inputs are finite; a program needn't handle non-finite values.
Results may differ from a plain program's by a relative error of at most 0.0023.
Values may be sent and summed in bfloat16 or wider, within the bound.
A program may use at most 64 MiB of HBM per device.

v0:
```python
import jax
import jax.numpy as jnp
from jax import lax
from jax.sharding import PartitionSpec as P

D = 7168
FF = 2048
CAP = 24
epsilon = 1e-06


def per_device(residual, attn_parts, norm_gain, routes, route_weights, w_gate, w_gate_q):
    n_expert = lax.axis_size("expert")
    tok_count = residual.shape[0]
    local_cols = residual.shape[1]
    top_count = routes.shape[1]
    gain_local = norm_gain.astype(jnp.float32)[None, :]
    gain_full = lax.all_gather(norm_gain, "tensor", tiled=True).astype(jnp.float32)[None, :]
    summed = lax.psum_scatter(
        attn_parts[0].astype(jnp.float32).astype(jnp.bfloat16),
        "tensor",
        scatter_dimension=1,
        tiled=True,
    ).astype(jnp.float32)
    hidden = (residual.astype(jnp.float32) + summed).astype(jnp.bfloat16)
    expert_ids = jnp.arange(n_expert, dtype=jnp.int32)
    flat_routes = routes.reshape(-1)
    one_hot = (flat_routes[:, None] == expert_ids[None, :]).astype(jnp.int32)
    earlier = jnp.cumsum(one_hot, axis=0) - one_hot
    slot_index = jnp.sum(earlier * one_hot, axis=1)
    target = flat_routes * CAP + slot_index
    load_counts = jnp.sum(one_hot, axis=0)
    slot_ids = jnp.arange(n_expert * CAP, dtype=jnp.int32)
    placing = (slot_ids[:, None] == target[None, :]).reshape(n_expert * CAP, tok_count, top_count)
    dispatch = jnp.sum(placing.astype(jnp.int32), axis=2).astype(jnp.bfloat16)
    outgoing = jnp.dot(dispatch, hidden, preferred_element_type=jnp.float32).astype(jnp.bfloat16)
    outgoing = outgoing.reshape(n_expert, CAP, local_cols)
    count_rows = jnp.broadcast_to(
        load_counts.astype(jnp.bfloat16)[:, None, None], (n_expert, 1, local_cols)
    )
    outgoing = jnp.concatenate([outgoing, count_rows], axis=1)
    arrived = lax.all_to_all(outgoing, "expert", split_axis=0, concat_axis=0, tiled=True)
    arrived_counts = arrived[:, CAP, 0].astype(jnp.float32)
    own_block = arrived[:, :CAP, :].reshape(n_expert * CAP, local_cols)
    column_block = lax.all_gather(own_block, "tensor", axis=1, tiled=True)
    wide = column_block.astype(jnp.float32)
    scaling = lax.rsqrt(jnp.sum(wide * wide, axis=1, keepdims=True) / D + epsilon)
    normed = (wide * scaling * gain_full).astype(jnp.bfloat16)
    normed_local = (own_block.astype(jnp.float32) * scaling * gain_local).astype(jnp.bfloat16)
    full_acc = jnp.dot(normed, w_gate[0], preferred_element_type=jnp.float32)
    quant_acc = jnp.dot(normed, w_gate_q[0], preferred_element_type=jnp.float32)
    block_squares = jnp.einsum(
        "rc,rc->c", normed_local, normed_local, preferred_element_type=jnp.float32
    )
    total_load = jnp.sum(arrived_counts)
    hess_local = 2.0 * block_squares / total_load
    difference = full_acc - quant_acc
    err_part = (jnp.sum(difference * difference, axis=1) / FF).reshape(n_expert, 1, CAP)
    pow_part = (jnp.sum(full_acc * full_acc, axis=1) / FF).reshape(n_expert, 1, CAP)
    slots = lax.psum(jnp.concatenate([err_part, pow_part], axis=1), "tensor")
    expert_total = jnp.sum(slots[:, 0]) / (jnp.sum(slots[:, 1]) + epsilon)
    back = lax.all_to_all(slots, "expert", split_axis=0, concat_axis=0, tiled=True)
    token_err = jnp.take(back[:, 0].reshape(-1), target).reshape(tok_count, top_count)
    token_pow = jnp.take(back[:, 1].reshape(-1), target).reshape(tok_count, top_count)
    ratios = token_err / (token_pow + epsilon)
    token_error = jnp.sum(route_weights * ratios, axis=1)
    return (token_error, expert_total.reshape(1), hess_local.reshape(1, local_cols))


def solution(mesh):
    placed = (
        P("expert", "tensor"),
        P("tensor", "expert", None),
        P("tensor"),
        P("expert", None),
        P("expert", None),
        P("expert", None, "tensor"),
        P("expert", None, "tensor"),
    )
    return jax.shard_map(
        per_device,
        mesh=mesh,
        in_specs=placed,
        out_specs=(P("expert"), P("expert"), P("expert", "tensor")),
        check_vma=False,
    )
```

profile of v0, /device:TPU:2, one launch (start us, length us, event | category | flops | bytes accessed | tf_op | source)
XLA Modules:
  0.0 279.3 jit_solution(10890716168880705273)
XLA Ops:
  7.2 2.8 copy.51
  10.4 1.2 reduce-window.6
  11.5 0.2 slice_reduce_fusion
  11.8 0.2 fusion.28
  12.2 0.5 convert_reduce_fusion
  12.7 65.0 %reduce-scatter.4.cloned.1.call-done = bf16[448,64]{1,0:T(8,128)(2,1)} async-done(((bf16[7168,64]{1,0:T(8,128)(2,1)}), bf16[448,64]{1,0:T(8,128)(2,1)}) %reduce-scatter.4.cloned.1.call-update) | async-done | bytes 57360
  77.8 1.0 copy.52
  78.8 0.4 convolution_convert_fusion
  79.2 0.3 copy.41
  79.5 0.1 broadcast_in_dim.6
  79.6 0.2 pad_maximum_fusion
  79.8 34.8 %all_to_all.10 = bf16[32,25,448]{2,1,0:T(8,128)(2,1)S(1)} all-to-all(bf16[32,25,448]{2,1,0:T(8,128)(2,1)S(1)} %pad_maximum_fusion), channel_id=1, replica_groups=mesh['expert'=32,'tensor'=16] {'expert'}, dimensions={0} | all-to-all | bytes 1433600 | tf_op jit(solution)/shard_map/all_to_all | solution.py:42
  114.5 1.0 copy-done.3
  115.6 1.2 copy.42
  116.8 1.3 dynamic-slice
  118.8 0.3 dynamic-update-slice
  119.0 51.5 %all-reduce = bf16[7168]{0:T(1024)(128)(2,1)S(1)} all-reduce(bf16[7168]{0:T(1024)(128)(2,1)S(1)} %dynamic-update-slice), channel_id=1, replica_groups=mesh['expert'=32,'tensor'=16] {'tensor'}, use_global_device_ids=true, to_apply=%add | all-reduce | flops 7168 | bytes 28672
  170.6 1.5 fusion.30
  172.1 13.0 %all-gather.2.cloned.1.call-done = bf16[768,7168]{0,1:T(8,128)(2,1)} async-done(((bf16[768,448]{0,1:T(8,128)(2,1)}), bf16[768,7168]{0,1:T(8,128)(2,1)}) %all-gather.2.cloned.1.call-update) | async-done | bytes 11010064 | tf_op jit(solution)/shard_map/all_gather | solution.py:45
  185.1 6.5 %fusion = f32[768]{0:T(1024)S(1)} fusion(bf16[768,7168]{0,1:T(8,128)(2,1)} %all-gather.2.cloned.1.call-done), kind=kLoop, calls=%fused_computation.4 | loop fusion | flops 16514304 | bytes 11013120 | tf_op jit(solution)/shard_map/reduce_sum | solution.py:47
  191.6 1.5 fusion.9
  193.1 3.3 %multiply_reduce_fusion = (f32[768]{0:T(1024)S(1)}, f32[768,128]{0,1:T(8,128)S(1)}) fusion(bf16[1,7168,128]{2,1,0:T(8,128)(2,1)S(1)} %copy-done, bf16[768,7168]{0,1:T(8,128)(2,1)S(1)} %copy-done.1, f32[7168]{0:T(1024)S(1)} %convert_element_type.66, f32[768]{0:T(1024)S(1)} %add_rsqrt_fusion), kind=kOutput, calls=%fused_computation.22 | convolution fusion | flops 1431502080 | bytes 13273088 | tf_op jit(solution)/shard_map/dot_general | solution.py:50
  196.5 3.4 %fusion.20 = f32[768]{0:T(1024)S(1)} fusion(f32[768,128]{0,1:T(8,128)S(1)} %get-tuple-element.11, bf16[1,7168,128]{2,1,0:T(8,128)(2,1)S(1)} %copy-done.8, bf16[768,7168]{0,1:T(8,128)(2,1)S(1)} %copy-done.1, f32[7168]{0:T(1024)S(1)} %convert_element_type.66, f32[768]{0:T(1024)S(1)} %add_rsqrt_fusion), kind=kOutput, calls=%fused_computation.19 | convolution fusion | flops 1431600384 | bytes 13273088 | tf_op jit(solution)/shard_map/dot_general | solution.py:51
  200.0 46.7 %psum.7 = f32[32,2,24]{2,0,1:T(8,128)S(1)} all-reduce(f32[32,2,24]{2,0,1:T(8,128)S(1)} %pad_maximum_fusion.1), channel_id=1, replica_groups=mesh['expert'=32,'tensor'=16] {'tensor'}, use_global_device_ids=true, to_apply=%region_9.10 | all-reduce | flops 1536 | bytes 12288 | tf_op jit(solution)/shard_map/psum | solution.py:60
  246.7 0.6 copy.43
  247.4 9.8 %all-to-all-start.1 = ((f32[32,2,24]{2,1,0:T(2,128)}), f32[32,2,24]{2,1,0:T(2,128)S(1)}, u32[]{:S(2)}, u32[]{:S(2)}) async-start(f32[32,2,24]{2,1,0:T(2,128)} %copy.43), calls=%async_computation.1 | async-start | bytes 65536 | tf_op jit(solution)/shard_map/all_to_all | solution.py:62
  257.1 1.2 multiply_divide_fusion
  258.4 0.6 slice_reduce_fusion.1
  260.3 5.5 %all-to-all-done.1 = f32[32,2,24]{2,1,0:T(2,128)S(1)} async-done(((f32[32,2,24]{2,1,0:T(2,128)}), f32[32,2,24]{2,1,0:T(2,128)S(1)}, u32[]{:S(2)}, u32[]{:S(2)}) %all-to-all-start.1) | async-done | bytes 6176 | tf_op jit(solution)/shard_map/all_to_all | solution.py:62
  266.0 2.3 gather_fusion
  268.3 2.3 gather_fusion.1
  270.7 0.6 multiply_reduce_fusion.1
  (50 shorter events, 1.4 us)
Async XLA Ops:
  7.2 186.0 %copy-start = (bf16[1,7168,128]{2,1,0:T(8,128)(2,1)S(1)}, bf16[1,7168,128]{2,1,0:T(8,128)(2,1)}, u32[]{:S(2)}) copy-start(bf16[1,7168,128]{2,1,0:T(8,128)(2,1)} %param.14) | copy-start | bytes 5505028
  7.2 70.6 %reduce-scatter.4.cloned.1.call-start = ((), (), s32[]{:S(2)}) async-start(), calls=%async_computation.4 | async-start | bytes 1949696
  7.2 2.8 %copy-start.5 = (s32[64,8]{0,1:T(8,128)S(1)}, s32[64,8]{0,1:T(8,128)}, u32[]{:S(2)}) copy-start(s32[64,8]{0,1:T(8,128)} %param.12) | copy-start | bytes 6148
  10.0 68.8 %copy-start.4 = (bf16[64,448]{1,0:T(8,128)(2,1)S(1)}, bf16[64,448]{1,0:T(8,128)(2,1)}, u32[]{:S(2)}) copy-start(bf16[64,448]{1,0:T(8,128)(2,1)} %param.9) | copy-start | bytes 172036
  10.0 175.1 %all-gather.2.cloned.1.call-start = ((), (), s32[]{:S(2)}) async-start(), calls=%async_computation.3 | async-start | bytes 11698176 | tf_op jit(solution)/shard_map/all_gather | solution.py:45
  114.5 1.0 copy-start.3
  115.5 1.3 copy-start.7
  115.5 55.0 %copy-start.6 = (f32[64,8]{0,1:T(8,128)S(1)}, f32[64,8]{0,1:T(8,128)}, u32[]{:S(2)}) copy-start(f32[64,8]{0,1:T(8,128)} %param.13) | copy-start | bytes 6148
  115.6 56.5 %copy-start.2 = (bf16[32,24,448]{2,1,0:T(8,128)(2,1)}, bf16[32,24,448]{2,1,0:T(8,128)(2,1)S(1)}, u32[]{:S(2)}) copy-start(bf16[32,24,448]{2,1,0:T(8,128)(2,1)S(1)} %slice.37) | copy-start | bytes 2064388
  185.1 8.0 %copy-start.1 = (bf16[768,7168]{0,1:T(8,128)(2,1)S(1)}, bf16[768,7168]{0,1:T(8,128)(2,1)}, u32[]{:S(2)}) copy-start(bf16[768,7168]{0,1:T(8,128)(2,1)} %all-gather.2.cloned.1.call-done) | copy-start | bytes 33030148
  193.1 3.3 %copy-start.8 = (bf16[1,7168,128]{2,1,0:T(8,128)(2,1)S(1)}, bf16[1,7168,128]{2,1,0:T(8,128)(2,1)}, u32[]{:S(2)}) copy-start(bf16[1,7168,128]{2,1,0:T(8,128)(2,1)} %param.15) | copy-start | bytes 5505028
  247.4 18.4 %all-to-all-start.1 = ((f32[32,2,24]{2,1,0:T(2,128)}), f32[32,2,24]{2,1,0:T(2,128)S(1)}, u32[]{:S(2)}, u32[]{:S(2)}) async-start(f32[32,2,24]{2,1,0:T(2,128)} %copy.43), calls=%async_computation.1 | async-start | bytes 65536 | tf_op jit(solution)/shard_map/all_to_all | solution.py:62
Sparse Core Ops, SparseCore 0:
  10.8 66.8 reduce-scatter.3
  116.9 68.1 all-gather.1
where the time goes:
time: 280 us; the launch traced here: 279 us
  blocking collectives  133 us (48%)
  waiting for transfers between devices  83.6 us (30%)
  between operations  17.4 us (6%)
  local copies, waits for them, and re-layouts  14.4 us (5%)
  other arithmetic  14.1 us (5%)
  starting transfers between devices  9.86 us (4%)
  matrix products  7.03 us (3%)
    unnamed x3, waiting for transfers between devices  65.1 us
    unnamed x1, blocking collectives  51.5 us
    psum x1, blocking collectives, per_device(): slots = lax.psum(jnp.concatenate([err_part, pow_part], axis=1), 'tensor')  46.7 us
    all_to_all x1, blocking collectives, per_device(): lax.all_to_all(outgoing, 'expert', split_axis=0, concat_axis=0, tiled=True)  34.8 us
    all_gather x1, waiting for transfers between devices, per_device(): column_block = lax.all_gather(own_block, 'tensor', axis=1, tiled=True)  13 us
    all_to_all x1, starting transfers between devices, per_device(): lax.all_to_all(slots, 'expert', split_axis=0, concat_axis=0, tiled=True)  9.77 us
    reduce_sum x1, other arithmetic, per_device(): jnp.sum(wide * wide, axis=1, keepdims=True) / D + epsilon  6.51 us
    unnamed x25, local copies, waits for them, and re-layouts  6.44 us
  transfers between devices with their start and end apart: 3, of which 3 were waited for; matrix products, arithmetic and copies ran while one was open for 3% of the time, Pallas kernels for 0%

commit v1 on v0

--- a/solution.py
+++ b/solution.py
@@ -42,7 +42,26 @@
     arrived = lax.all_to_all(outgoing, "expert", split_axis=0, concat_axis=0, tiled=True)
     arrived_counts = arrived[:, CAP, 0].astype(jnp.float32)
     own_block = arrived[:, :CAP, :].reshape(n_expert * CAP, local_cols)
-    column_block = lax.all_gather(own_block, "tensor", axis=1, tiled=True)
+    size, mine, width = (lax.axis_size("tensor"), lax.axis_index("tensor"), own_block.shape[1])
+    forward = [(i, (i + 1) % size) for i in range(size)]
+    backward = [(i, (i - 1) % size) for i in range(size)]
+    whole = jnp.zeros(
+        (*own_block.shape[:1], size * width, *own_block.shape[1 + 1 :]), own_block.dtype
+    )
+    whole = lax.dynamic_update_slice_in_dim(whole, own_block, mine * width, axis=1)
+    from_left = from_right = own_block
+    half = size // 2
+    for step in range(1, half + 1):
+        from_left = lax.ppermute(from_left, "tensor", forward)
+        whole = lax.dynamic_update_slice_in_dim(
+            whole, from_left, (mine - step) % size * width, axis=1
+        )
+        if step < size - half:
+            from_right = lax.ppermute(from_right, "tensor", backward)
+            whole = lax.dynamic_update_slice_in_dim(
+                whole, from_right, (mine + step) % size * width, axis=1
+            )
+    column_block = whole
     wide = column_block.astype(jnp.float32)
     scaling = lax.rsqrt(jnp.sum(wide * wide, axis=1, keepdims=True) / D + epsilon)
     normed = (wide * scaling * gain_full).astype(jnp.bfloat16)

time: 280 us -> 504 us (1.80)
  local copies, waits for them, and re-layouts: 14.4 us -> 175 us
  waiting for transfers between devices: 83.6 us -> 129 us
  starting transfers between devices: 9.86 us -> 23.2 us
    dynamic_update_slice x0 -> x16, local copies, waits for them, and re-layouts: none -> 132 us  [the longest x8 65.3 us: per_device(): lax.dynamic_update_slice_in_dim(whole, from_left, (mine - step) % size *...]
    ppermute x0 -> x15, waiting for transfers between devices: none -> 60.1 us  [the longest x8 60.1 us: per_device(): from_left = lax.ppermute(from_left, 'tensor', forward)]
    ppermute x0 -> x15, local copies, waits for them, and re-layouts: none -> 19.5 us  [the longest x8 11 us: per_device(): from_left = lax.ppermute(from_left, 'tensor', forward)]
    ppermute x0 -> x15, starting transfers between devices: none -> 17.6 us  [the longest x7 17.6 us: per_device(): from_right = lax.ppermute(from_right, 'tensor', backward)]
    all_gather x1 -> x0, waiting for transfers between devices: 13 us -> none  [per_device(): column_block = lax.all_gather(own_block, 'tensor', axis=1, tiled=True)]
    broadcast_in_dim x0 -> x1, local copies, waits for them, and re-layouts: none -> 5.53 us  [per_device(): jnp.zeros((*own_block.shape[:1], size * width, *own_block.shape[1 + 1:]),...]
    unnamed x25 -> x41, local copies, waits for them, and re-layouts: 6.44 us -> 10.4 us
    unnamed x3 -> x2, waiting for transfers between devices: 65.1 us -> 63.8 us
  transfers between devices with their start and end apart: 3 -> 17, of which waited for: 3 -> 9; matrix products, arithmetic and copies ran while one was open for 3% -> 31% of each run, Pallas kernels for 0% -> 0%
where the time goes in v1:
time: 504 us; the launch traced here: 500 us
  local copies, waits for them, and re-layouts  175 us (35%)
  blocking collectives  130 us (26%)
  waiting for transfers between devices  129 us (26%)
  starting transfers between devices  23.2 us (5%)
  between operations  17.6 us (3%)
  other arithmetic  14.7 us (3%)
  matrix products  9.11 us (2%)
    dynamic_update_slice x8, local copies, waits for them, and re-layouts, per_device(): lax.dynamic_update_slice_in_dim(whole, from_left, (mine - step) % size *...  65.3 us
    unnamed x2, waiting for transfers between devices  63.8 us
    ppermute x8, waiting for transfers between devices, per_device(): from_left = lax.ppermute(from_left, 'tensor', forward)  60.1 us
    dynamic_update_slice x7, local copies, waits for them, and re-layouts, per_device(): lax.dynamic_update_slice_in_dim(whole, from_right, (mine + step) % size *...  58.3 us
    unnamed x1, blocking collectives  49.8 us
    psum x1, blocking collectives, per_device(): slots = lax.psum(jnp.concatenate([err_part, pow_part], axis=1), 'tensor')  45.7 us
    all_to_all x1, blocking collectives, per_device(): lax.all_to_all(outgoing, 'expert', split_axis=0, concat_axis=0, tiled=True)  34.9 us
    ppermute x7, starting transfers between devices, per_device(): from_right = lax.ppermute(from_right, 'tensor', backward)  17.6 us
  transfers between devices with their start and end apart: 17, of which 9 were waited for; matrix products, arithmetic and copies ran while one was open for 31% of the time, Pallas kernels for 0%

profile of v1, /device:TPU:2, one launch (start us, length us, event | category | flops | bytes accessed | tf_op | source)
XLA Modules:
  0.0 499.5 jit_solution(2733963562140236434)
XLA Ops:
  14.1 63.8 %reduce-scatter.4.cloned.1.call-done = bf16[448,64]{1,0:T(8,128)(2,1)} async-done(((bf16[7168,64]{1,0:T(8,128)(2,1)}), bf16[448,64]{1,0:T(8,128)(2,1)}) %reduce-scatter.4.cloned.1.call-update) | async-done | bytes 57360
  80.6 34.9 %all_to_all.10 = bf16[32,25,448]{2,1,0:T(8,128)(2,1)} all-to-all(bf16[32,25,448]{2,1,0:T(8,128)(2,1)S(1)} %pad_maximum_fusion), channel_id=1, replica_groups=mesh['expert'=32,'tensor'=16] {'expert'}, dimensions={0} | all-to-all | bytes 1433600 | tf_op jit(solution)/shard_map/all_to_all | solution.py:42
  119.9 8.6 %collective-permute-done = bf16[768,448]{0,1:T(8,128)(2,1)S(1)} collective-permute-done((bf16[768,448]{0,1:T(8,128)(2,1)S(1)}, bf16[768,448]{0,1:T(8,128)(2,1)S(1)}, u32[]{:S(2)}, u32[]{:S(2)}) %collective-permute-start) | collective-permute-done | bytes 688160 | tf_op jit(solution)/shard_map/ppermute | solution.py:55
  131.6 8.5 %collective-permute-done.2 = bf16[768,448]{0,1:T(8,128)(2,1)S(1)} collective-permute-done((bf16[768,448]{0,1:T(8,128)(2,1)S(1)}, bf16[768,448]{0,1:T(8,128)(2,1)S(1)}, u32[]{:S(2)}, u32[]{:S(2)}) %collective-permute-start.2) | collective-permute-done | bytes 688160 | tf_op jit(solution)/shard_map/ppermute | solution.py:55
  143.9 8.6 %collective-permute-done.4 = bf16[768,448]{0,1:T(8,128)(2,1)S(1)} collective-permute-done((bf16[768,448]{0,1:T(8,128)(2,1)S(1)}, bf16[768,448]{0,1:T(8,128)(2,1)S(1)}, u32[]{:S(2)}, u32[]{:S(2)}) %collective-permute-start.4) | collective-permute-done | bytes 688160 | tf_op jit(solution)/shard_map/ppermute | solution.py:55
  155.5 8.6 %collective-permute-done.6 = bf16[768,448]{0,1:T(8,128)(2,1)S(1)} collective-permute-done((bf16[768,448]{0,1:T(8,128)(2,1)S(1)}, bf16[768,448]{0,1:T(8,128)(2,1)S(1)}, u32[]{:S(2)}, u32[]{:S(2)}) %collective-permute-start.6) | collective-permute-done | bytes 688160 | tf_op jit(solution)/shard_map/ppermute | solution.py:55
  167.1 8.6 %collective-permute-done.8 = bf16[768,448]{0,1:T(8,128)(2,1)S(1)} collective-permute-done((bf16[768,448]{0,1:T(8,128)(2,1)S(1)}, bf16[768,448]{0,1:T(8,128)(2,1)S(1)}, u32[]{:S(2)}, u32[]{:S(2)}) %collective-permute-start.8) | collective-permute-done | bytes 688160 | tf_op jit(solution)/shard_map/ppermute | solution.py:55
  178.7 8.6 %collective-permute-done.10 = bf16[768,448]{0,1:T(8,128)(2,1)S(1)} collective-permute-done((bf16[768,448]{0,1:T(8,128)(2,1)S(1)}, bf16[768,448]{0,1:T(8,128)(2,1)S(1)}, u32[]{:S(2)}, u32[]{:S(2)}) %collective-permute-start.10) | collective-permute-done | bytes 688160 | tf_op jit(solution)/shard_map/ppermute | solution.py:55
  190.4 8.6 %collective-permute-done.12 = bf16[768,448]{0,1:T(8,128)(2,1)} collective-permute-done((bf16[768,448]{0,1:T(8,128)(2,1)S(1)}, bf16[768,448]{0,1:T(8,128)(2,1)}, u32[]{:S(2)}, u32[]{:S(2)}) %collective-permute-start.12) | collective-permute-done | bytes 688160 | tf_op jit(solution)/shard_map/ppermute | solution.py:55
  201.2 49.8 %all-reduce = bf16[7168]{0:T(1024)(128)(2,1)S(1)} all-reduce(bf16[7168]{0:T(1024)(128)(2,1)S(1)} %dynamic-update-slice), channel_id=1, replica_groups=mesh['expert'=32,'tensor'=16] {'tensor'}, use_global_device_ids=true, to_apply=%add | all-reduce | flops 7168 | bytes 28672
  251.1 5.5 %broadcast_in_dim.8 = bf16[768,7168]{1,0:T(8,128)(2,1)} broadcast(bf16[]{:T(256)} %constant.114.clone.1), dimensions={} | broadcast | bytes 11010050 | tf_op jit(solution)/shard_map/broadcast_in_dim | solution.py:48
  256.6 7.9 %dynamic_update_slice.48 = bf16[768,7168]{1,0:T(8,128)(2,1)} dynamic-update-slice(bf16[768,7168]{1,0:T(8,128)(2,1)} %broadcast_in_dim.8, bf16[768,448]{1,0:T(8,128)(2,1)S(1)} %bitcast.40, s32[]{:T(128)} %constant.116.clone.1, s32[]{:T(128)S(6)} %select_n.118) | dynamic-update-slice | bytes 1376260 | tf_op jit(solution)/shard_map/dynamic_update_slice | solution.py:51
  267.3 8.0 %dynamic_update_slice.49 = bf16[768,7168]{1,0:T(8,128)(2,1)} dynamic-update-slice(bf16[768,7168]{1,0:T(8,128)(2,1)} %dynamic_update_slice.48, bf16[768,448]{1,0:T(8,128)(2,1)S(1)} %copy.75, s32[]{:T(128)} %constant.116.clone.1, s32[]{:T(128)S(6)} %select_n.120) | dynamic-update-slice | bytes 1376260 | tf_op jit(solution)/shard_map/dynamic_update_slice | solution.py:56
  276.7 8.7 %dynamic_update_slice.50 = bf16[768,7168]{1,0:T(8,128)(2,1)} dynamic-update-slice(bf16[768,7168]{1,0:T(8,128)(2,1)} %dynamic_update_slice.49, bf16[768,448]{1,0:T(8,128)(2,1)S(1)} %copy.77, s32[]{:T(128)} %constant.116.clone.1, s32[]{:T(128)S(6)} %select_n.122) | dynamic-update-slice | bytes 1376260 | tf_op jit(solution)/shard_map/dynamic_update_slice | solution.py:61
  286.8 7.7 %dynamic_update_slice.51 = bf16[768,7168]{1,0:T(8,128)(2,1)} dynamic-update-slice(bf16[768,7168]{1,0:T(8,128)(2,1)} %dynamic_update_slice.50, bf16[768,448]{1,0:T(8,128)(2,1)S(1)} %copy.78, s32[]{:T(128)} %constant.116.clone.1, s32[]{:T(128)S(6)} %select_n.124) | dynamic-update-slice | bytes 1376260 | tf_op jit(solution)/shard_map/dynamic_update_slice | solution.py:56
  295.9 7.9 %dynamic_update_slice.52 = bf16[768,7168]{1,0:T(8,128)(2,1)} dynamic-update-slice(bf16[768,7168]{1,0:T(8,128)(2,1)} %dynamic_update_slice.51, bf16[768,448]{1,0:T(8,128)(2,1)S(1)} %copy.79, s32[]{:T(128)} %constant.116.clone.1, s32[]{:T(128)S(6)} %select_n.126) | dynamic-update-slice | bytes 1376260 | tf_op jit(solution)/shard_map/dynamic_update_slice | solution.py:61
  305.2 8.7 %dynamic_update_slice.53 = bf16[768,7168]{1,0:T(8,128)(2,1)} dynamic-update-slice(bf16[768,7168]{1,0:T(8,128)(2,1)} %dynamic_update_slice.52, bf16[768,448]{1,0:T(8,128)(2,1)S(1)} %copy.80, s32[]{:T(128)} %constant.116.clone.1, s32[]{:T(128)S(6)} %select_n.128) | dynamic-update-slice | bytes 1376260 | tf_op jit(solution)/shard_map/dynamic_update_slice | solution.py:56
  315.3 8.7 %dynamic_update_slice.54 = bf16[768,7168]{1,0:T(8,128)(2,1)} dynamic-update-slice(bf16[768,7168]{1,0:T(8,128)(2,1)} %dynamic_update_slice.53, bf16[768,448]{1,0:T(8,128)(2,1)S(1)} %copy.81, s32[]{:T(128)} %constant.116.clone.1, s32[]{:T(128)S(6)} %select_n.130) | dynamic-update-slice | bytes 1376260 | tf_op jit(solution)/shard_map/dynamic_update_slice | solution.py:61
  325.4 7.8 %dynamic_update_slice.55 = bf16[768,7168]{1,0:T(8,128)(2,1)} dynamic-update-slice(bf16[768,7168]{1,0:T(8,128)(2,1)} %dynamic_update_slice.54, bf16[768,448]{1,0:T(8,128)(2,1)S(1)} %copy.82, s32[]{:T(128)} %constant.116.clone.1, s32[]{:T(128)S(6)} %select_n.132) | dynamic-update-slice | bytes 1376260 | tf_op jit(solution)/shard_map/dynamic_update_slice | solution.py:56
  333.5 7.8 %dynamic_update_slice.56 = bf16[768,7168]{1,0:T(8,128)(2,1)} dynamic-update-slice(bf16[768,7168]{1,0:T(8,128)(2,1)} %dynamic_update_slice.55, bf16[768,448]{1,0:T(8,128)(2,1)S(1)} %copy.83, s32[]{:T(128)} %constant.116.clone.1, s32[]{:T(128)S(6)} %select_n.134) | dynamic-update-slice | bytes 1376260 | tf_op jit(solution)/shard_map/dynamic_update_slice | solution.py:61
  342.7 8.7 %dynamic_update_slice.57 = bf16[768,7168]{1,0:T(8,128)(2,1)} dynamic-update-slice(bf16[768,7168]{1,0:T(8,128)(2,1)} %dynamic_update_slice.56, bf16[768,448]{1,0:T(8,128)(2,1)S(1)} %copy.84, s32[]{:T(128)} %constant.116.clone.1, s32[]{:T(128)S(6)} %select_n.136) | dynamic-update-slice | bytes 1376260 | tf_op jit(solution)/shard_map/dynamic_update_slice | solution.py:56
  352.7 8.7 %dynamic_update_slice.58 = bf16[768,7168]{1,0:T(8,128)(2,1)} dynamic-update-slice(bf16[768,7168]{1,0:T(8,128)(2,1)} %dynamic_update_slice.57, bf16[768,448]{1,0:T(8,128)(2,1)S(1)} %copy.85, s32[]{:T(128)} %constant.116.clone.1, s32[]{:T(128)S(6)} %select_n.138) | dynamic-update-slice | bytes 1376260 | tf_op jit(solution)/shard_map/dynamic_update_slice | solution.py:61
  362.8 7.9 %dynamic_update_slice.59 = bf16[768,7168]{1,0:T(8,128)(2,1)} dynamic-update-slice(bf16[768,7168]{1,0:T(8,128)(2,1)} %dynamic_update_slice.58, bf16[768,448]{1,0:T(8,128)(2,1)S(1)} %copy.86, s32[]{:T(128)} %constant.116.clone.1, s32[]{:T(128)S(6)} %select_n.140) | dynamic-update-slice | bytes 1376260 | tf_op jit(solution)/shard_map/dynamic_update_slice | solution.py:56
  372.0 7.9 %dynamic_update_slice.60 = bf16[768,7168]{1,0:T(8,128)(2,1)} dynamic-update-slice(bf16[768,7168]{1,0:T(8,128)(2,1)} %dynamic_update_slice.59, bf16[768,448]{1,0:T(8,128)(2,1)S(1)} %copy.87, s32[]{:T(128)} %constant.116.clone.1, s32[]{:T(128)S(6)} %select_n.142) | dynamic-update-slice | bytes 1376260 | tf_op jit(solution)/shard_map/dynamic_update_slice | solution.py:61
  381.3 8.7 %dynamic_update_slice.61 = bf16[768,7168]{1,0:T(8,128)(2,1)} dynamic-update-slice(bf16[768,7168]{1,0:T(8,128)(2,1)} %dynamic_update_slice.60, bf16[768,448]{1,0:T(8,128)(2,1)S(1)} %copy.88, s32[]{:T(128)} %constant.116.clone.1, s32[]{:T(128)S(6)} %select_n.144) | dynamic-update-slice | bytes 1376260 | tf_op jit(solution)/shard_map/dynamic_update_slice | solution.py:56
  391.3 8.7 %dynamic_update_slice.62 = bf16[768,7168]{1,0:T(8,128)(2,1)} dynamic-update-slice(bf16[768,7168]{1,0:T(8,128)(2,1)} %dynamic_update_slice.61, bf16[768,448]{1,0:T(8,128)(2,1)S(1)} %copy.89, s32[]{:T(128)} %constant.116.clone.1, s32[]{:T(128)S(6)} %select_n.146) | dynamic-update-slice | bytes 1376260 | tf_op jit(solution)/shard_map/dynamic_update_slice | solution.py:61
  401.4 7.9 %dynamic_update_slice.63 = bf16[768,7168]{1,0:T(8,128)(2,1)} dynamic-update-slice(bf16[768,7168]{1,0:T(8,128)(2,1)} %dynamic_update_slice.62, bf16[768,448]{1,0:T(8,128)(2,1)S(1)} %copy.90, s32[]{:T(128)} %constant.116.clone.1, s32[]{:T(128)S(6)} %select_n.148) | dynamic-update-slice | bytes 1376260 | tf_op jit(solution)/shard_map/dynamic_update_slice | solution.py:56
  409.3 6.5 %fusion = f32[768]{0:T(1024)S(1)} fusion(bf16[768,7168]{1,0:T(8,128)(2,1)} %dynamic_update_slice.63), kind=kLoop, calls=%fused_computation.4 | loop fusion | flops 16514304 | bytes 11013120 | tf_op jit(solution)/shard_map/reduce_sum | solution.py:66
  421.2 4.0 fusion.20
  425.4 45.7 %psum.7 = f32[32,2,24]{2,0,1:T(8,128)S(1)} all-reduce(f32[32,2,24]{2,0,1:T(8,128)S(1)} %pad_maximum_fusion.1), channel_id=1, replica_groups=mesh['expert'=32,'tensor'=16] {'tensor'}, use_global_device_ids=true, to_apply=%region_9.10 | all-reduce | flops 1536 | bytes 12288 | tf_op jit(solution)/shard_map/psum | solution.py:79
  471.7 5.6 %all-to-all-start.1 = ((f32[32,2,24]{2,1,0:T(2,128)}), f32[32,2,24]{2,1,0:T(2,128)S(1)}, u32[]{:S(2)}, u32[]{:S(2)}) async-start(f32[32,2,24]{2,1,0:T(2,128)} %copy.91), calls=%async_computation.1 | async-start | bytes 65536 | tf_op jit(solution)/shard_map/all_to_all | solution.py:81
  480.4 5.5 %all-to-all-done.1 = f32[32,2,24]{2,1,0:T(2,128)S(1)} async-done(((f32[32,2,24]{2,1,0:T(2,128)}), f32[32,2,24]{2,1,0:T(2,128)S(1)}, u32[]{:S(2)}, u32[]{:S(2)}) %all-to-all-start.1) | async-done | bytes 6176 | tf_op jit(solution)/shard_map/all_to_all | solution.py:81
  (125 shorter events, 69.2 us)
Async XLA Ops:
  7.2 410.1 %copy-start = (bf16[1,7168,128]{2,1,0:T(8,128)(2,1)S(1)}, bf16[1,7168,128]{2,1,0:T(8,128)(2,1)}, u32[]{:S(2)}) copy-start(bf16[1,7168,128]{2,1,0:T(8,128)(2,1)} %param.14) | copy-start | bytes 5505028
  7.2 191.8 %copy-start.15 = (bf16[448]{0:T(512)(128)(2,1)S(1)}, bf16[448]{0:T(512)(128)(2,1)}, u32[]{:S(2)}) copy-start(bf16[448]{0:T(512)(128)(2,1)} %param.11) | copy-start | bytes 2692
  7.2 243.8 %copy-start.14 = (f32[64,8]{0,1:T(8,128)S(1)}, f32[64,8]{0,1:T(8,128)}, u32[]{:S(2)}) copy-start(f32[64,8]{0,1:T(8,128)} %param.13) | copy-start | bytes 6148
  7.2 70.6 %reduce-scatter.4.cloned.1.call-start = ((), (), s32[]{:S(2)}) async-start(), calls=%async_computation.3 | async-start | bytes 1949696
  116.7 170.1 %copy-start.2 = (bf16[32,24,448]{2,1,0:T(8,128)(2,1)}, bf16[32,24,448]{2,1,0:T(8,128)(2,1)S(1)}, u32[]{:S(2)}) copy-start(bf16[32,24,448]{2,1,0:T(8,128)(2,1)S(1)} %slice.37) | copy-start | bytes 2064388
  117.0 11.6 %collective-permute-start = (bf16[768,448]{0,1:T(8,128)(2,1)S(1)}, bf16[768,448]{0,1:T(8,128)(2,1)S(1)}, u32[]{:S(2)}, u32[]{:S(2)}) collective-permute-start(bf16[768,448]{0,1:T(8,128)(2,1)S(1)} %copy.74), channel_id=1, source_target_pairs={{0,1},{1,2},{2,3},{3,4},{4,5},{5,6},{6,7},{7,8},{8,9},{9,10},{10,1... | collective-permute-start | bytes 2064392 | tf_op jit(solution)/shard_map/ppermute | solution.py:55
  117.0 11.6 %collective-permute-start.1 = (bf16[768,448]{0,1:T(8,128)(2,1)S(1)}, bf16[768,448]{0,1:T(8,128)(2,1)}, u32[]{:S(2)}, u32[]{:S(2)}) collective-permute-start(bf16[768,448]{0,1:T(8,128)(2,1)S(1)} %copy.74), channel_id=1, source_target_pairs={{0,15},{1,0},{2,1},{3,2},{4,3},{5,4},{6,5},{7,6},{8,7},{9,8},{10,9... | collective-permute-start | bytes 2064392 | tf_op jit(solution)/shard_map/ppermute | solution.py:60
  128.5 24.0 %copy-start.4 = (bf16[768,448]{0,1:T(8,128)(2,1)}, bf16[768,448]{0,1:T(8,128)(2,1)S(1)}, u32[]{:S(2)}) copy-start(bf16[768,448]{0,1:T(8,128)(2,1)S(1)} %collective-permute-done) | copy-start | bytes 2064388
  128.5 11.6 %collective-permute-start.2 = (bf16[768,448]{0,1:T(8,128)(2,1)S(1)}, bf16[768,448]{0,1:T(8,128)(2,1)S(1)}, u32[]{:S(2)}, u32[]{:S(2)}) collective-permute-start(bf16[768,448]{0,1:T(8,128)(2,1)S(1)} %collective-permute-done), channel_id=1, source_target_pairs={{0,1},{1,2},{2,3},{3,4},{4,5},{5,6},{6,7},{7,8},{8,9},{9,10},{10,1... | collective-permute-start | bytes 2064392 | tf_op jit(solution)/shard_map/ppermute | solution.py:55
  128.6 12.4 %collective-permute-start.3 = (bf16[768,448]{0,1:T(8,128)(2,1)}, bf16[768,448]{0,1:T(8,128)(2,1)S(1)}, u32[]{:S(2)}, u32[]{:S(2)}) collective-permute-start(bf16[768,448]{0,1:T(8,128)(2,1)} %collective-permute-done.1), channel_id=1, source_target_pairs={{0,15},{1,0},{2,1},{3,2},{4,3},{5,4},{6,5},{7,6},{8,7},{9,8},{10,9... | collective-permute-start | bytes 2064392 | tf_op jit(solution)/shard_map/ppermute | solution.py:60
  141.0 11.6 %collective-permute-start.4 = (bf16[768,448]{0,1:T(8,128)(2,1)S(1)}, bf16[768,448]{0,1:T(8,128)(2,1)S(1)}, u32[]{:S(2)}, u32[]{:S(2)}) collective-permute-start(bf16[768,448]{0,1:T(8,128)(2,1)S(1)} %collective-permute-done.2), channel_id=1, source_target_pairs={{0,1},{1,2},{2,3},{3,4},{4,5},{5,6},{6,7},{7,8},{8,9},{9,10},{10,1... | collective-permute-start | bytes 2064392 | tf_op jit(solution)/shard_map/ppermute | solution.py:55
  141.0 11.6 %copy-start.5 = (bf16[768,448]{0,1:T(8,128)(2,1)}, bf16[768,448]{0,1:T(8,128)(2,1)S(1)}, u32[]{:S(2)}) copy-start(bf16[768,448]{0,1:T(8,128)(2,1)S(1)} %collective-permute-done.3) | copy-start | bytes 2064388
  141.0 11.6 %collective-permute-start.5 = (bf16[768,448]{0,1:T(8,128)(2,1)S(1)}, bf16[768,448]{0,1:T(8,128)(2,1)S(1)}, u32[]{:S(2)}, u32[]{:S(2)}) collective-permute-start(bf16[768,448]{0,1:T(8,128)(2,1)S(1)} %collective-permute-done.3), channel_id=1, source_target_pairs={{0,15},{1,0},{2,1},{3,2},{4,3},{5,4},{6,5},{7,6},{8,7},{9,8},{10,9... | collective-permute-start | bytes 2064392 | tf_op jit(solution)/shard_map/ppermute | solution.py:60
  152.5 11.6 %collective-permute-start.6 = (bf16[768,448]{0,1:T(8,128)(2,1)S(1)}, bf16[768,448]{0,1:T(8,128)(2,1)S(1)}, u32[]{:S(2)}, u32[]{:S(2)}) collective-permute-start(bf16[768,448]{0,1:T(8,128)(2,1)S(1)} %collective-permute-done.4), channel_id=1, source_target_pairs={{0,1},{1,2},{2,3},{3,4},{4,5},{5,6},{6,7},{7,8},{8,9},{9,10},{10,1... | collective-permute-start | bytes 2064392 | tf_op jit(solution)/shard_map/ppermute | solution.py:55
  153.4 10.7 %copy-start.7 = (bf16[768,448]{0,1:T(8,128)(2,1)}, bf16[768,448]{0,1:T(8,128)(2,1)S(1)}, u32[]{:S(2)}) copy-start(bf16[768,448]{0,1:T(8,128)(2,1)S(1)} %collective-permute-done.5) | copy-start | bytes 2064388
  153.4 10.7 %collective-permute-start.7 = (bf16[768,448]{0,1:T(8,128)(2,1)S(1)}, bf16[768,448]{0,1:T(8,128)(2,1)S(1)}, u32[]{:S(2)}, u32[]{:S(2)}) collective-permute-start(bf16[768,448]{0,1:T(8,128)(2,1)S(1)} %collective-permute-done.5), channel_id=1, source_target_pairs={{0,15},{1,0},{2,1},{3,2},{4,3},{5,4},{6,5},{7,6},{8,7},{9,8},{10,9... | collective-permute-start | bytes 2064392 | tf_op jit(solution)/shard_map/ppermute | solution.py:60
  164.1 0.9 copy-start.8
  164.1 11.6 %collective-permute-start.8 = (bf16[768,448]{0,1:T(8,128)(2,1)S(1)}, bf16[768,448]{0,1:T(8,128)(2,1)S(1)}, u32[]{:S(2)}, u32[]{:S(2)}) collective-permute-start(bf16[768,448]{0,1:T(8,128)(2,1)S(1)} %collective-permute-done.6), channel_id=1, source_target_pairs={{0,1},{1,2},{2,3},{3,4},{4,5},{5,6},{6,7},{7,8},{8,9},{9,10},{10,1... | collective-permute-start | bytes 2064392 | tf_op jit(solution)/shard_map/ppermute | solution.py:55
  165.0 10.7 %copy-start.9 = (bf16[768,448]{0,1:T(8,128)(2,1)}, bf16[768,448]{0,1:T(8,128)(2,1)S(1)}, u32[]{:S(2)}) copy-start(bf16[768,448]{0,1:T(8,128)(2,1)S(1)} %collective-permute-done.7) | copy-start | bytes 2064388
  165.0 10.7 %collective-permute-start.9 = (bf16[768,448]{0,1:T(8,128)(2,1)S(1)}, bf16[768,448]{0,1:T(8,128)(2,1)S(1)}, u32[]{:S(2)}, u32[]{:S(2)}) collective-permute-start(bf16[768,448]{0,1:T(8,128)(2,1)S(1)} %collective-permute-done.7), channel_id=1, source_target_pairs={{0,15},{1,0},{2,1},{3,2},{4,3},{5,4},{6,5},{7,6},{8,7},{9,8},{10,9... | collective-permute-start | bytes 2064392 | tf_op jit(solution)/shard_map/ppermute | solution.py:60
  175.7 0.9 copy-start.11
  175.7 11.6 %collective-permute-start.10 = (bf16[768,448]{0,1:T(8,128)(2,1)S(1)}, bf16[768,448]{0,1:T(8,128)(2,1)S(1)}, u32[]{:S(2)}, u32[]{:S(2)}) collective-permute-start(bf16[768,448]{0,1:T(8,128)(2,1)S(1)} %collective-permute-done.8), channel_id=1, source_target_pairs={{0,1},{1,2},{2,3},{3,4},{4,5},{5,6},{6,7},{7,8},{8,9},{9,10},{10,1... | collective-permute-start | bytes 2064392 | tf_op jit(solution)/shard_map/ppermute | solution.py:55
  176.6 10.7 %copy-start.12 = (bf16[768,448]{0,1:T(8,128)(2,1)}, bf16[768,448]{0,1:T(8,128)(2,1)S(1)}, u32[]{:S(2)}) copy-start(bf16[768,448]{0,1:T(8,128)(2,1)S(1)} %collective-permute-done.9) | copy-start | bytes 2064388
  176.6 10.7 %collective-permute-start.11 = (bf16[768,448]{0,1:T(8,128)(2,1)S(1)}, bf16[768,448]{0,1:T(8,128)(2,1)}, u32[]{:S(2)}, u32[]{:S(2)}) collective-permute-start(bf16[768,448]{0,1:T(8,128)(2,1)S(1)} %collective-permute-done.9), channel_id=1, source_target_pairs={{0,15},{1,0},{2,1},{3,2},{4,3},{5,4},{6,5},{7,6},{8,7},{9,8},{10,9... | collective-permute-start | bytes 2064392 | tf_op jit(solution)/shard_map/ppermute | solution.py:60
  187.3 0.9 copy-start.13
  187.3 11.7 %collective-permute-start.12 = (bf16[768,448]{0,1:T(8,128)(2,1)S(1)}, bf16[768,448]{0,1:T(8,128)(2,1)}, u32[]{:S(2)}, u32[]{:S(2)}) collective-permute-start(bf16[768,448]{0,1:T(8,128)(2,1)S(1)} %collective-permute-done.10), channel_id=1, source_target_pairs={{0,1},{1,2},{2,3},{3,4},{4,5},{5,6},{6,7},{7,8},{8,9},{9,10},{10,1... | collective-permute-start | bytes 2064392 | tf_op jit(solution)/shard_map/ppermute | solution.py:55
  188.1 201.8 %collective-permute-start.13 = (bf16[768,448]{0,1:T(8,128)(2,1)}, bf16[768,448]{0,1:T(8,128)(2,1)}, u32[]{:S(2)}, u32[]{:S(2)}) collective-permute-start(bf16[768,448]{0,1:T(8,128)(2,1)} %collective-permute-done.11), channel_id=1, source_target_pairs={{0,15},{1,0},{2,1},{3,2},{4,3},{5,4},{6,5},{7,6},{8,7},{9,8},{10,9... | collective-permute-start | bytes 2064392 | tf_op jit(solution)/shard_map/ppermute | solution.py:60
  199.0 201.1 %collective-permute-start.14 = (bf16[768,448]{0,1:T(8,128)(2,1)}, bf16[768,448]{0,1:T(8,128)(2,1)}, u32[]{:S(2)}, u32[]{:S(2)}) collective-permute-start(bf16[768,448]{0,1:T(8,128)(2,1)} %collective-permute-done.12), channel_id=1, source_target_pairs={{0,1},{1,2},{2,3},{3,4},{4,5},{5,6},{6,7},{7,8},{8,9},{9,10},{10,1... | collective-permute-start | bytes 2064392 | tf_op jit(solution)/shard_map/ppermute | solution.py:55
  294.5 38.7 %copy-start.10 = (bf16[768,448]{0,1:T(8,128)(2,1)S(1)}, bf16[768,448]{0,1:T(8,128)(2,1)}, u32[]{:S(2)}) copy-start(bf16[768,448]{0,1:T(8,128)(2,1)} %copy-done.9) | copy-start | bytes 2064388
  409.3 8.0 %copy-start.1 = (bf16[768,7168]{1,0:T(8,128)(2,1)S(1)}, bf16[768,7168]{1,0:T(8,128)(2,1)}, u32[]{:S(2)}) copy-start(bf16[768,7168]{1,0:T(8,128)(2,1)} %dynamic_update_slice.63) | copy-start | bytes 33030148
  417.3 3.9 copy-start.16
  471.7 14.2 %all-to-all-start.1 = ((f32[32,2,24]{2,1,0:T(2,128)}), f32[32,2,24]{2,1,0:T(2,128)S(1)}, u32[]{:S(2)}, u32[]{:S(2)}) async-start(f32[32,2,24]{2,1,0:T(2,128)} %copy.91), calls=%async_computation.1 | async-start | bytes 65536 | tf_op jit(solution)/shard_map/all_to_all | solution.py:81
  (2 other events, 1.7 us)
Sparse Core Ops, SparseCore 0:
  10.9 66.9 reduce-scatter.3
